TPU v7x, 32 devices: a whole 2x2x4 slice. The times are simulated.
32 devices in a mesh: seq: 16 (over z, x, core), head: 2 (over y).
Axes of the slice: x: 2, y: 2, z: 4, core: 2. Of those that a mesh axis runs over, the one named last changes fastest.
Arguments:
- qkv: bfloat16 [3, 8192, 4096], P(None, ('seq', 'head')), may hold values from -6 to 6
- send_rows: int32 [16, 16, 40], P('seq'), may hold values from -1 to 511, as said below
- recv_pos: int32 [16, 16, 40], P('seq'), may hold values from -1 to 511, as said below
- req_lengths: int32 [4], replicated, may hold values from 1 to 4096, 8192 in all
- norm_gain: float32 [4096], P('head'), may hold values from 0.5 to 1.5
Outputs:
- attn_out: bfloat16 [8192, 4096], P('seq', 'head')
Inputs may be any that keep to these rules, and one draw needn't show every extreme that they name: send_rows[l, o, c] is a row of loader group l (rows l * 512 to l * 512 + 511 of qkv, counted from the group's first) sent to owner o in slot c, or -1 for an empty slot; used slots come first. Every row of a group is sent exactly once. At most 40 rows go from one group to one owner, and in every draw some pairs carry exactly 40, so that every group sends and every owner receives 40 rows from one pair. The number of rows from group l to owner o depends only on (o - l) modulo the number of groups. recv_pos[o, l, c] is the position within owner o's block of 512 packed positions where slot c from group l lands, and -1 exactly where send_rows[l, o, c] is -1; every position of a block is filled exactly once.
All inputs are finite; a program needn't handle non-finite values.
Results may differ from a plain program's by a relative error of at most 0.003.
Values may be sent and summed in bfloat16 or wider, within the bound.
No kernel may reach another device: no remote copies, remote signals or barrier semaphores. Data moves between devices by JAX's collectives and lax.ppermute only.
A program may use at most 128 MiB of HBM per device.

v0:
```python
import jax
import jax.numpy as jnp
from jax import lax
from jax.sharding import PartitionSpec as P

HEAD_DIM = 128
norm_eps = 1e-06


def prefix(shard, axis, combine, identity):
    length, position = (lax.axis_size(axis), lax.axis_index(axis))
    everything = jax.tree.map(lambda part: lax.all_gather(part, axis), shard)
    start = jax.tree.map(
        lambda part, zero: jnp.broadcast_to(jnp.asarray(zero, part.dtype), part.shape),
        shard,
        identity,
    )

    def lap(k, before):
        reached = k < position
        new = combine(before, jax.tree.map(lambda part: part[k], everything))
        return jax.tree.map(lambda a, b: jnp.where(reached, a, b), new, before)

    return lax.fori_loop(0, length, lap, start)


def place_rows(incoming, land_rows, tok_rows):
    row_width = incoming.shape[-1]
    planes = incoming.shape[0]
    flat_rows = incoming.reshape(planes, -1, row_width)
    land_index = jnp.where(land_rows < 0, tok_rows, land_rows).reshape(-1)
    blank_rows = jnp.zeros((planes, tok_rows, row_width), incoming.dtype)
    return blank_rows.at[:, land_index].set(flat_rows, mode="drop")


def carry_combine(earlier, later):
    return (later[0] + (1.0 - later[1]) * earlier[0], jnp.maximum(earlier[1], later[1]))


def on_device(qkv, send_rows, recv_pos, req_lengths, norm_gain):
    seq_count = lax.axis_size("seq")
    slot_count = send_rows.shape[2]
    pick_rows = jnp.maximum(send_rows[0], 0).reshape(-1)
    land_rows = recv_pos[0]
    grouped = lax.all_to_all(qkv, "head", split_axis=2, concat_axis=1, tiled=True)
    outgoing = jnp.take(grouped, pick_rows, axis=1).reshape(
        3, seq_count, slot_count, grouped.shape[2]
    )
    arrived = lax.all_to_all(outgoing, "seq", split_axis=1, concat_axis=1, tiled=True)
    packed = place_rows(arrived, land_rows, grouped.shape[1])
    query, keys, values = (packed[0], packed[1], packed[2])
    tok_rows = keys.shape[0]
    head_count = keys.shape[1] // HEAD_DIM
    first_row = lax.axis_index("seq") * tok_rows
    req_ends = jnp.cumsum(req_lengths)
    req_starts = req_ends - req_lengths
    positions = first_row + jnp.arange(tok_rows, dtype=jnp.int32)
    segment = jnp.sum((req_starts[None, :] <= positions[:, None]).astype(jnp.int32), axis=1) - 1
    prev_segment = jnp.sum((req_starts < first_row).astype(jnp.int32)) - 1
    inside = jnp.any((req_starts >= first_row) & (req_starts < first_row + tok_rows))
    has_start = jnp.where(inside, 1.0, 0.0).astype(jnp.float32)
    carried_mask = segment == prev_segment
    tail_mask = segment == segment[tok_rows - 1]
    causal = (positions[None, :] <= positions[:, None]) & (segment[None, :] == segment[:, None])
    tail_keys = jnp.where(tail_mask[:, None], keys, jnp.zeros_like(keys))
    update = jnp.einsum(
        "shd,she->hde",
        tail_keys.reshape(tok_rows, head_count, HEAD_DIM),
        values.reshape(tok_rows, head_count, HEAD_DIM),
        preferred_element_type=jnp.float32,
    )
    identity = (jnp.zeros_like(update), jnp.zeros((), jnp.float32))
    carried_pair = prefix((update, has_start), "seq", carry_combine, identity)
    carried = carried_pair[0]
    outputs = []
    for number in range(head_count):
        columns = slice(number * HEAD_DIM, (number + 1) * HEAD_DIM)
        query_head = query[:, columns]
        key_head = keys[:, columns]
        value_head = values[:, columns]
        scores = lax.dot_general(
            query_head, key_head, (((1,), (1,)), ((), ())), preferred_element_type=jnp.float32
        )
        weights = jnp.where(causal, scores, 0.0).astype(jnp.bfloat16)
        local_term = jnp.dot(weights, value_head, preferred_element_type=jnp.float32)
        carried_term = jnp.dot(
            query_head.astype(jnp.float32),
            carried[number],
            precision=lax.Precision.HIGHEST,
            preferred_element_type=jnp.float32,
        )
        raw_out = local_term + jnp.where(carried_mask[:, None], carried_term, 0.0)
        inv_rms = lax.rsqrt(jnp.mean(raw_out * raw_out, axis=1, keepdims=True) + norm_eps)
        outputs.append((raw_out * inv_rms * norm_gain[columns][None, :]).astype(jnp.bfloat16))
    return jnp.concatenate(outputs, axis=1)


def solution(mesh):
    return jax.shard_map(
        on_device,
        mesh=mesh,
        in_specs=(
            P(None, ("seq", "head"), None),
            P("seq", None, None),
            P("seq", None, None),
            P(),
            P("head"),
        ),
        out_specs=P("seq", "head"),
        check_vma=False,
    )
```

profile of v0, /device:TPU:0, one launch (start us, length us, event | category | flops | bytes accessed | tf_op | source)
XLA Modules:
  0.0 782.3 jit_solution(8094631923778563405)
XLA Ops:
  6.5 13.1 %copy.40 = bf16[3,256,4096]{1,0,2:T(4,128)(2,1)} copy(bf16[3,256,4096]{2,1,0:T(8,128)(2,1)} %param.7) | data formatting | bytes 12582912 | tf_op args[0]
  19.6 7.1 all-to-all-start
  26.8 93.7 %all-to-all-done = bf16[3,256,4096]{1,0,2:T(4,128)(2,1)} async-done(((bf16[3,256,4096]{1,0,2:T(4,128)(2,1)}), bf16[3,256,4096]{1,0,2:T(4,128)(2,1)}, u32[]{:S(2)}, u32[]{:S(2)}) %all-to-all-start) | async-done | bytes 6291488 | tf_op jit(solution)/shard_map/all_to_all | solution.py:45
  120.6 7.0 copy.41
  127.5 8.7 %copy.42 = bf16[3,2,256,2048]{3,2,1,0:T(8,128)(2,1)} copy(bf16[3,2,256,2048]{2,3,1,0:T(8,128)(2,1)} %bitcast.90) | data formatting | bytes 12582912 | tf_op jit(solution)/shard_map/all_to_all | solution.py:45
  136.2 11.5 %copy.43 = bf16[3,512,2048]{2,0,1:T(4,128)(2,1)} copy(bf16[3,512,2048]{2,1,0:T(8,128)(2,1)} %bitcast.91) | data formatting | bytes 12582912 | tf_op jit(solution)/shard_map/all_to_all | solution.py:45
  147.7 24.7 %gather_fusion = bf16[640,3,2048]{2,1,0:T(4,128)(2,1)} fusion(bf16[3,512,2048]{2,0,1:T(4,128)(2,1)} %copy.43, s32[1024]{0:T(1024)S(1)} %pad_clamp_fusion), kind=kCustom, calls=%fused_computation | custom fusion | bytes 15731200 | tf_op jit(solution)/shard_map/jit(_take)/gather | solution.py:46
  172.5 16.3 %copy_select_fusion = bf16[3,16,40,2048]{3,2,0,1:T(8,128)(2,1)} fusion(bf16[3,16,40,2048]{3,0,2,1:T(4,128)(2,1)} %bitcast.88, pred[16,40]{1,0:T(8,128)(4,1)S(1)} %compare_bitcast_fusion), kind=kLoop, calls=%fused_computation.4 | loop fusion | flops 3932160 | bytes 15729280 | tf_op jit(solution)/shard_map/jit(_take)/select_n | solution.py:46
  188.7 6.2 all-to-all-start.1
  198.7 137.9 %all-to-all-done.1 = bf16[3,16,40,2048]{3,2,0,1:T(8,128)(2,1)} async-done(((bf16[3,16,40,2048]{3,2,0,1:T(8,128)(2,1)}), bf16[3,16,40,2048]{3,2,0,1:T(8,128)(2,1)}, u32[]{:S(2)}, u32[]{:S(2)}) %all-to-all-start.1) | async-done | bytes 7864352 | tf_op jit(solution)/shard_map/all_to_all | solution.py:49
  336.6 4.2 copy.45
  340.8 25.5 %copy.46 = bf16[640,3,2048]{2,1,0:T(4,128)(2,1)} copy(bf16[640,3,2048]{2,0,1:T(8,128)(2,1)S(1)} %bitcast.89) | data formatting | bytes 15728640 | tf_op jit(solution)/shard_map/reshape | solution.py:30
  366.3 7.6 broadcast_in_dim.178
  373.9 85.0 %scatter_fusion = bf16[3,512,2048]{2,0,1:T(4,128)(2,1)} fusion(bf16[3,512,2048]{2,0,1:T(4,128)(2,1)} %broadcast_in_dim.178, s32[640]{0:T(1024)S(1)} %fusion.213, bf16[640,3,2048]{2,1,0:T(4,128)(2,1)} %copy.46), kind=kCustom, calls=%fused_computation.1 | custom fusion | bytes 23595520 | tf_op jit(solution)/shard_map/scatter | solution.py:33
  459.0 20.8 %fusion.232 = (bf16[1,512,2048]{2,0,1:T(2,128)(2,1)}, bf16[1,512,2048]{2,0,1:T(2,128)(2,1)}, bf16[1,512,2048]{2,0,1:T(2,128)(2,1)}) fusion(bf16[3,512,2048]{2,0,1:T(4,128)(2,1)} %scatter_fusion), kind=kLoop, calls=%fused_computation.301 | loop fusion | bytes 12582912 | tf_op jit(solution)/shard_map/slice | solution.py:51
  479.8 9.0 %copy.47 = bf16[1,512,2048]{1,2,0:T(8,128)(2,1)S(1)} copy(bf16[1,512,2048]{2,0,1:T(2,128)(2,1)} %get-tuple-element.130) | data formatting | bytes 4194304 | tf_op jit(solution)/shard_map/slice | solution.py:51
  488.8 10.5 %copy.48 = bf16[1,512,2048]{1,2,0:T(8,128)(2,1)} copy(bf16[1,512,2048]{2,0,1:T(2,128)(2,1)} %get-tuple-element.131) | data formatting | bytes 4194304 | tf_op jit(solution)/shard_map/slice | solution.py:51
  499.3 3.3 fusion.1
  504.5 63.3 %all-reduce = f32[16]{0:T(128)S(1)} all-reduce(f32[16]{0:T(128)S(1)} %dynamic-update-slice), channel_id=1, replica_groups=mesh['seq'=16,'head'=2] {'seq'}, use_global_device_ids=true, to_apply=%add | all-reduce | flops 16 | bytes 128
  567.8 3.6 copy.59
  571.5 6.9 copy_bitcast_fusion
  578.4 80.6 %all-gather.3.cloned.1.call-done = f32[256,128,128]{2,1,0:T(8,128)} async-done(((f32[16,128,128]{2,1,0:T(8,128)}), f32[256,128,128]{2,1,0:T(8,128)}) %all-gather.3.cloned.1.call-update) | async-done | bytes 16777232 | tf_op jit(solution)/shard_map/all_gather | solution.py:12
  658.9 54.5 %while.14 = (s32[]{:T(128)}, f32[16,128,128]{2,1,0:T(8,128)S(1)}, s32[]{:T(128)}, f32[16,16,128,128]{3,2,1,0:T(8,128)}, f32[16]{0:T(128)S(1)}, /*index=5*/s32[]{:T(128)}, f32[1]{0:T(128)}, s32[]{:T(128)}) while((s32[]{:T(128)}, f32[16,128,128]{2,1,0:T(8,128)S(1)}, s32[]{:T(128)}, f32[16,16,128,128]{3,2,1,0:T(8,128)}, ...), condition=%wide.region_6.7_spmd.clone, body=%wide.region_5.6_spmd.clone.sunk | while | flops 1048581 | bytes 3145873 | solution.py:24
  731.6 2.4 multiply_reduce_fusion.4
  740.9 2.3 multiply_reduce_fusion.8
  745.5 2.3 multiply_reduce_fusion.10
  747.8 2.3 multiply_reduce_fusion.11
  750.1 2.3 multiply_reduce_fusion.12
  752.4 2.3 multiply_reduce_fusion.13
  754.7 2.3 multiply_reduce_fusion.14
  757.0 2.3 multiply_reduce_fusion.15
  772.7 2.4 copy.50
  (169 shorter events, 89.0 us)
Async XLA Ops:
  19.6 7.1 copy-start.25
  19.6 100.9 %all-to-all-start = ((bf16[3,256,4096]{1,0,2:T(4,128)(2,1)}), bf16[3,256,4096]{1,0,2:T(4,128)(2,1)}, u32[]{:S(2)}, u32[]{:S(2)}) async-start(bf16[3,256,4096]{1,0,2:T(4,128)(2,1)} %copy.40), calls=%async_computation | async-start | bytes 16777216 | tf_op jit(solution)/shard_map/all_to_all | solution.py:45
  188.7 6.3 copy-start.28
  188.7 7.8 %copy-start.26 = (s32[1,16,40]{2,1,0:T(8,128)S(1)}, s32[1,16,40]{2,1,0:T(8,128)}, u32[]{:S(2)}) copy-start(s32[1,16,40]{2,1,0:T(8,128)} %param.9) | copy-start | bytes 7684
  188.7 147.8 %all-to-all-start.1 = ((bf16[3,16,40,2048]{3,2,0,1:T(8,128)(2,1)}), bf16[3,16,40,2048]{3,2,0,1:T(8,128)(2,1)}, u32[]{:S(2)}, u32[]{:S(2)}) async-start(bf16[3,16,40,2048]{3,2,0,1:T(8,128)(2,1)} %copy_select_fusion), calls=%async_computation.1 | async-start | bytes 15728640 | tf_op jit(solution)/shard_map/all_to_all | solution.py:49
  195.0 464.0 %all-gather.3.cloned.1.call-start = ((), (), s32[]{:S(2)}) async-start(), calls=%async_computation.2 | async-start | bytes 17825792 | tf_op jit(solution)/shard_map/all_gather | solution.py:12
  499.3 3.3 copy-start.29
  499.3 68.5 %copy-start.27 = (f32[2048]{0:T(1024)S(1)}, f32[2048]{0:T(1024)}, u32[]{:S(2)}) copy-start(f32[2048]{0:T(1024)} %param.11) | copy-start | bytes 24580
  567.8 3.7 copy-start
  729.9 4.1 copy-start.24
  731.6 4.7 copy-start.23
  734.0 4.6 copy-start.22
  736.3 4.6 copy-start.21
  738.6 4.6 copy-start.20
  740.9 4.6 copy-start.19
  743.2 4.6 copy-start.18
  745.5 4.6 copy-start.17
  747.8 4.6 copy-start.16
  750.1 4.6 copy-start.15
  752.4 4.6 copy-start.14
  754.7 4.6 copy-start.13
  757.0 4.6 copy-start.12
  759.3 4.5 copy-start.11
  766.0 5.5 copy-start.10
  766.1 5.6 copy-start.7
  766.1 5.7 copy-start.6
  766.1 5.8 copy-start.4
  766.1 5.9 copy-start.3
  766.1 6.0 copy-start.2
  767.3 5.0 copy-start.1
  769.4 3.0 copy-start.9
  770.5 2.0 copy-start.8
  (1 other events, 1.0 us)
Sparse Core Ops, SparseCore 0:
  502.7 156.1 all-gather.2
where the time goes:
time: 794 us; the launch traced here: 782 us
  waiting for transfers between devices  312 us (39%)
  local copies, waits for them, and re-layouts  253 us (32%)
  blocking collectives  63.3 us (8%)
  other arithmetic  59.2 us (7%)
  matrix products  55.6 us (7%)
  between operations  15.6 us (2%)
  starting transfers between devices  13.3 us (2%)
  loops' own time  10.4 us (1%)
    all_to_all x1, waiting for transfers between devices, on_device(): lax.all_to_all(outgoing, 'seq', split_axis=1, concat_axis=1, tiled=True)  138 us
    all_to_all x1, waiting for transfers between devices, on_device(): lax.all_to_all(qkv, 'head', split_axis=2, concat_axis=1, tiled=True)  93.7 us
    scatter x1, local copies, waits for them, and re-layouts, place_rows(): return blank_rows.at[:, land_index].set(flat_rows, mode='drop')  85 us
    all_gather x1, waiting for transfers between devices, prefix(): everything = jax.tree.map(lambda part: lax.all_gather(part, axis), shard)  80.6 us
    unnamed x1, blocking collectives  63.3 us
    slice x3, local copies, waits for them, and re-layouts, on_device(): query, keys, values = (packed[0], packed[1], packed[2])  40.3 us
    dot_general x16, matrix products, on_device(): jnp.dot(weights, value_head, preferred_element_type=jnp.float32)  35.8 us
    select_n x16, other arithmetic, lap(): return jax.tree.map(lambda a, b: jnp.where(reached, a, b), new, before)  34.2 us
  transfers between devices with their start and end apart: 3, of which 3 were waited for; matrix products, arithmetic and copies ran while one was open for 2% of the time, Pallas kernels for 0%

commit v1 on v0

--- a/solution.py
+++ b/solution.py
@@ -5,6 +5,20 @@
 
 HEAD_DIM = 128
 norm_eps = 1e-06
+
+
+def recover_sections(inp, out_dim, view):
+    z1, item_now = (inp.shape[:out_dim], inp.shape[out_dim + 1 :])
+    a_now = inp.reshape(*z1, view, -1, *item_now)
+    f_now = jnp.moveaxis(a_now, out_dim, 0)
+    return f_now
+
+
+def serve_sample(panel, array_dim):
+    e_next = list(panel.shape[1:])
+    e_next[array_dim] *= panel.shape[0]
+    u_next = jnp.moveaxis(panel, 0, array_dim).reshape(e_next)
+    return u_next
 
 
 def prefix(shard, axis, combine, identity):
@@ -46,7 +60,21 @@
     outgoing = jnp.take(grouped, pick_rows, axis=1).reshape(
         3, seq_count, slot_count, grouped.shape[2]
     )
-    arrived = lax.all_to_all(outgoing, "seq", split_axis=1, concat_axis=1, tiled=True)
+    step_out = lax.axis_size("seq")
+    field_out = lax.axis_index("seq")
+    fresh, piece_out = (step_out, field_out)
+    taken_in = recover_sections(outgoing, 1, fresh)
+    fields = [taken_in[piece_out]]
+    tick = 1
+    while tick < fresh:
+        arr_now = taken_in[piece_out ^ tick]
+        upper = lax.ppermute(
+            arr_now, axis_name="seq", perm=[(dd, dd ^ tick) for dd in range(fresh)]
+        )
+        fields.append(upper)
+        tick += 1
+    taken_in = jnp.stack(fields)[piece_out ^ jnp.arange(fresh)]
+    arrived = serve_sample(taken_in, 1)
     packed = place_rows(arrived, land_rows, grouped.shape[1])
     query, keys, values = (packed[0], packed[1], packed[2])
     tok_rows = keys.shape[0]

time: 794 us -> 833 us (1.049)
  starting transfers between devices: 13.3 us -> 70.3 us
  waiting for transfers between devices: 312 us -> 256 us
  local copies, waits for them, and re-layouts: 253 us -> 296 us
  other arithmetic: 59.2 us -> 50.6 us
    all_to_all x1 -> x0, waiting for transfers between devices: 138 us -> none  [on_device(): lax.all_to_all(outgoing, 'seq', split_axis=1, concat_axis=1, tiled=True)]
    ppermute x0 -> x15, waiting for transfers between devices: none -> 78.7 us  [on_device(): lax.ppermute(arr_now, axis_name='seq', perm=[(dd, dd ^ tick) for dd in ra...]
    ppermute x0 -> x15, starting transfers between devices: none -> 63.1 us  [on_device(): lax.ppermute(arr_now, axis_name='seq', perm=[(dd, dd ^ tick) for dd in ra...]
    another operation x0 -> x18, local copies, waits for them, and re-layouts: none -> 38.1 us  [the longest x1 25.3 us: place_rows(): flat_rows = incoming.reshape(planes, -1, row_width)]
    reshape x1 -> x0, local copies, waits for them, and re-layouts: 25.5 us -> none  [place_rows(): flat_rows = incoming.reshape(planes, -1, row_width)]
    gather x0 -> x1, local copies, waits for them, and re-layouts: none -> 17.6 us  [on_device(): taken_in = jnp.stack(fields)[piece_out ^ jnp.arange(fresh)]]
    unnamed x66 -> x81, local copies, waits for them, and re-layouts: 25 us -> 38 us
    select_n x1, other arithmetic: 16.3 us -> 7.52 us  [on_device(): jnp.take(grouped, pick_rows, axis=1)]
  transfers between devices with their start and end apart: 3 -> 17, of which waited for: 3 -> 8; matrix products, arithmetic and copies ran while one was open for 2% -> 4% of each run, Pallas kernels for 0% -> 0%
where the time goes in v1:
time: 833 us; the launch traced here: 820 us
  local copies, waits for them, and re-layouts  296 us (36%)
  waiting for transfers between devices  256 us (31%)
  starting transfers between devices  70.3 us (8%)
  blocking collectives  64.2 us (8%)
  matrix products  55.3 us (7%)
  other arithmetic  50.6 us (6%)
  between operations  16 us (2%)
  loops' own time  11.7 us (1%)
    all_to_all x1, waiting for transfers between devices, on_device(): lax.all_to_all(qkv, 'head', split_axis=2, concat_axis=1, tiled=True)  89.8 us
    all_gather x1, waiting for transfers between devices, prefix(): everything = jax.tree.map(lambda part: lax.all_gather(part, axis), shard)  87.7 us
    scatter x1, local copies, waits for them, and re-layouts, place_rows(): return blank_rows.at[:, land_index].set(flat_rows, mode='drop')  85.1 us
    ppermute x15, waiting for transfers between devices, on_device(): lax.ppermute(arr_now, axis_name='seq', perm=[(dd, dd ^ tick) for dd in ra...  78.7 us
    unnamed x1, blocking collectives  64.2 us
    ppermute x15, starting transfers between devices, on_device(): lax.ppermute(arr_now, axis_name='seq', perm=[(dd, dd ^ tick) for dd in ra...  63.1 us
    slice x3, local copies, waits for them, and re-layouts, on_device(): query, keys, values = (packed[0], packed[1], packed[2])  40.2 us
    unnamed x81, local copies, waits for them, and re-layouts  38 us
  transfers between devices with their start and end apart: 17, of which 8 were waited for; matrix products, arithmetic and copies ran while one was open for 4% of the time, Pallas kernels for 0%

profile of v1, /device:TPU:0, one launch (start us, length us, event | category | flops | bytes accessed | tf_op | source)
XLA Modules:
  0.0 820.1 jit_solution(6094621009104755735)
XLA Ops:
  6.5 13.1 %copy.80 = bf16[3,256,4096]{1,0,2:T(4,128)(2,1)} copy(bf16[3,256,4096]{2,1,0:T(8,128)(2,1)} %param.7) | data formatting | bytes 12582912 | tf_op args[0]
  19.6 7.1 all-to-all-start
  30.8 89.8 %all-to-all-done = bf16[3,256,4096]{1,0,2:T(4,128)(2,1)} async-done(((bf16[3,256,4096]{1,0,2:T(4,128)(2,1)}), bf16[3,256,4096]{1,0,2:T(4,128)(2,1)}, u32[]{:S(2)}, u32[]{:S(2)}) %all-to-all-start) | async-done | bytes 6291488 | tf_op jit(solution)/shard_map/all_to_all | solution.py:59
  120.6 7.0 copy.81
  127.5 8.7 %copy.82 = bf16[3,2,256,2048]{3,2,1,0:T(8,128)(2,1)} copy(bf16[3,2,256,2048]{2,3,1,0:T(8,128)(2,1)} %bitcast.174) | data formatting | bytes 12582912 | tf_op jit(solution)/shard_map/all_to_all | solution.py:59
  136.2 11.5 %copy.83 = bf16[3,512,2048]{2,0,1:T(4,128)(2,1)} copy(bf16[3,512,2048]{2,1,0:T(8,128)(2,1)} %bitcast.175) | data formatting | bytes 12582912 | tf_op jit(solution)/shard_map/all_to_all | solution.py:59
  147.7 24.3 %gather_fusion = bf16[640,3,2048]{2,1,0:T(4,128)(2,1)} fusion(bf16[3,512,2048]{2,0,1:T(4,128)(2,1)} %copy.83, s32[1024]{0:T(1024)S(1)} %pad_clamp_fusion.1), kind=kCustom, calls=%fused_computation | custom fusion | bytes 15731200 | tf_op jit(solution)/shard_map/jit(_take)/gather | solution.py:60
  172.0 7.5 broadcast_select_fusion
  179.5 6.5 constant_dynamic-slice_fusion
  196.5 2.6 collective-permute-start.5
  204.5 7.3 collective-permute-done.2
  211.8 2.7 collective-permute-start.7
  216.3 3.6 collective-permute-start.9
  220.7 26.5 %collective-permute-done.5 = bf16[3,1,40,2048]{3,2,0,1:T(8,128)(2,1)S(1)} collective-permute-done((bf16[3,1,40,2048]{3,2,0,1:T(8,128)(2,1)S(1)}, bf16[3,1,40,2048]{3,2,0,1:T(8,128)(2,1)S(1)}, u32[]{:S(2)}, u32[]{:S(2)}) %collective-permute-start.5) | collective-permute-done | bytes 491552 | tf_op jit(solution)/shard_map/ppermute | solution.py:71
  248.1 8.5 %collective-permute-done.6 = bf16[3,1,40,2048]{3,2,0,1:T(8,128)(2,1)S(1)} collective-permute-done((bf16[3,1,40,2048]{3,2,0,1:T(8,128)(2,1)S(1)}, bf16[3,1,40,2048]{3,2,0,1:T(8,128)(2,1)S(1)}, u32[]{:S(2)}, u32[]{:S(2)}) %collective-permute-start.6) | collective-permute-done | bytes 491552 | tf_op jit(solution)/shard_map/ppermute | solution.py:71
  261.8 42.6 %collective-permute-start.13 = (bf16[3,1,40,2048]{3,2,0,1:T(8,128)(2,1)S(1)}, bf16[3,1,40,2048]{3,2,0,1:T(8,128)(2,1)S(1)}, u32[]{:S(2)}, u32[]{:S(2)}) collective-permute-start(bf16[3,1,40,2048]{3,2,0,1:T(8,128)(2,1)S(1)} %bitcast.212), channel_id=1, source_target_pairs={{0,28},{2,30},{4,24},{6,26},{8,20},{10,22},{12,16},{14,18},{16,12}... | collective-permute-start | bytes 1474568 | tf_op jit(solution)/shard_map/ppermute | solution.py:71
  305.3 17.3 %collective-permute-done.9 = bf16[3,1,40,2048]{3,2,0,1:T(8,128)(2,1)S(1)} collective-permute-done((bf16[3,1,40,2048]{3,2,0,1:T(8,128)(2,1)S(1)}, bf16[3,1,40,2048]{3,2,0,1:T(8,128)(2,1)S(1)}, u32[]{:S(2)}, u32[]{:S(2)}) %collective-permute-start.9) | collective-permute-done | bytes 491552 | tf_op jit(solution)/shard_map/ppermute | solution.py:71
  326.0 16.9 %collective-permute-done.10 = bf16[3,1,40,2048]{3,2,0,1:T(8,128)(2,1)S(1)} collective-permute-done((bf16[3,1,40,2048]{3,2,0,1:T(8,128)(2,1)S(1)}, bf16[3,1,40,2048]{3,2,0,1:T(8,128)(2,1)S(1)}, u32[]{:S(2)}, u32[]{:S(2)}) %collective-permute-start.10) | collective-permute-done | bytes 491552 | tf_op jit(solution)/shard_map/ppermute | solution.py:71
  347.2 17.6 %gather_fusion.1 = bf16[16,3,40,2048]{3,2,1,0:T(8,128)(2,1)} fusion(bf16[16,3,40,2048]{3,2,1,0:T(8,128)(2,1)} %bitcast.39, s32[1024]{0:T(1024)S(1)} %pad_clamp_fusion), kind=kCustom, calls=%fused_computation.1 | custom fusion | bytes 15728704 | tf_op jit(solution)/shard_map/gather | solution.py:76
  364.7 4.2 copy.100
  368.9 25.3 %copy.101 = bf16[640,3,2048]{2,1,0:T(4,128)(2,1)} copy(bf16[640,3,2048]{2,0,1:T(8,128)(2,1)S(1)} %bitcast.173) | data formatting | bytes 15728640 | tf_op jit(solution)/shard_map/reshape;reshape | solution.py:44
  394.3 7.6 broadcast_in_dim.179
  401.9 85.1 %scatter_fusion = bf16[3,512,2048]{2,0,1:T(4,128)(2,1)} fusion(bf16[3,512,2048]{2,0,1:T(4,128)(2,1)} %broadcast_in_dim.179, s32[640]{0:T(1024)S(1)} %fusion.213, bf16[640,3,2048]{2,1,0:T(4,128)(2,1)} %copy.101), kind=kCustom, calls=%fused_computation.2 | custom fusion | bytes 23595520 | tf_op jit(solution)/shard_map/scatter | solution.py:47
  487.0 20.8 %fusion.233 = (bf16[1,512,2048]{2,0,1:T(2,128)(2,1)}, bf16[1,512,2048]{2,0,1:T(2,128)(2,1)}, bf16[1,512,2048]{2,0,1:T(2,128)(2,1)}) fusion(bf16[3,512,2048]{2,0,1:T(4,128)(2,1)} %scatter_fusion), kind=kLoop, calls=%fused_computation.352 | loop fusion | bytes 12582912 | tf_op jit(solution)/shard_map/slice | solution.py:79
  507.7 9.0 %copy.102 = bf16[1,512,2048]{1,2,0:T(8,128)(2,1)S(1)} copy(bf16[1,512,2048]{2,0,1:T(2,128)(2,1)} %get-tuple-element.146) | data formatting | bytes 4194304 | tf_op jit(solution)/shard_map/slice | solution.py:79
  516.7 10.5 %copy.103 = bf16[1,512,2048]{1,2,0:T(8,128)(2,1)} copy(bf16[1,512,2048]{2,0,1:T(2,128)(2,1)} %get-tuple-element.147) | data formatting | bytes 4194304 | tf_op jit(solution)/shard_map/slice | solution.py:79
  527.2 3.3 fusion.1
  532.7 64.2 %all-reduce = f32[16]{0:T(128)S(1)} all-reduce(f32[16]{0:T(128)S(1)} %dynamic-update-slice), channel_id=1, replica_groups=mesh['seq'=16,'head'=2] {'seq'}, use_global_device_ids=true, to_apply=%add | all-reduce | flops 16 | bytes 128
  596.9 3.6 copy.129
  600.5 6.9 copy_bitcast_fusion
  607.4 87.7 %all-gather.3.cloned.1.call-done = f32[256,128,128]{2,1,0:T(8,128)} async-done(((f32[16,128,128]{2,1,0:T(8,128)}), f32[256,128,128]{2,1,0:T(8,128)}) %all-gather.3.cloned.1.call-update) | async-done | bytes 16777232 | tf_op jit(solution)/shard_map/all_gather | solution.py:26
  695.1 56.6 %while.14 = (s32[]{:T(128)}, f32[16,128,128]{2,1,0:T(8,128)S(1)}, s32[]{:T(128)}, f32[16,16,128,128]{3,2,1,0:T(8,128)}, f32[16]{0:T(128)S(1)}, /*index=5*/s32[]{:T(128)}, f32[1]{0:T(128)}, s32[]{:T(128)}) while((s32[]{:T(128)}, f32[16,128,128]{2,1,0:T(8,128)S(1)}, s32[]{:T(128)}, f32[16,16,128,128]{3,2,1,0:T(8,128)}, ...), condition=%wide.region_6.7_spmd.clone, body=%wide.region_5.6_spmd.clone.sunk | while | flops 1048581 | bytes 3145873 | solution.py:38
  (232 shorter events, 143.2 us)
Async XLA Ops:
  19.6 7.2 copy-start.28
  19.6 8.8 %copy-start.26 = (s32[1,16,40]{2,1,0:T(8,128)S(1)}, s32[1,16,40]{2,1,0:T(8,128)}, u32[]{:S(2)}) copy-start(s32[1,16,40]{2,1,0:T(8,128)} %param.9) | copy-start | bytes 7684
  19.6 8.8 %copy-start.25 = (s32[1,16,40]{2,1,0:T(8,128)S(1)}, s32[1,16,40]{2,1,0:T(8,128)}, u32[]{:S(2)}) copy-start(s32[1,16,40]{2,1,0:T(8,128)} %param.8) | copy-start | bytes 7684
  19.6 101.0 %all-to-all-start = ((bf16[3,256,4096]{1,0,2:T(4,128)(2,1)}), bf16[3,256,4096]{1,0,2:T(4,128)(2,1)}, u32[]{:S(2)}, u32[]{:S(2)}) async-start(bf16[3,256,4096]{1,0,2:T(4,128)(2,1)} %copy.80), calls=%async_computation | async-start | bytes 16777216 | tf_op jit(solution)/shard_map/all_to_all | solution.py:59
  26.7 668.4 %all-gather.3.cloned.1.call-start = ((), (), s32[]{:S(2)}) async-start(), calls=%async_computation.1 | async-start | bytes 17825792 | tf_op jit(solution)/shard_map/all_gather | solution.py:26
  186.4 10.0 %collective-permute-start = (bf16[3,1,40,2048]{3,2,0,1:T(8,128)(2,1)S(1)}, bf16[3,1,40,2048]{3,2,0,1:T(8,128)(2,1)S(1)}, u32[]{:S(2)}, u32[]{:S(2)}) collective-permute-start(bf16[3,1,40,2048]{3,2,0,1:T(8,128)(2,1)S(1)} %bitcast.224), channel_id=1, source_target_pairs={{0,2},{2,0},{4,6},{6,4},{8,10},{10,8},{12,14},{14,12},{16,18},{18,... | collective-permute-start | bytes 1474568 | tf_op jit(solution)/shard_map/ppermute | solution.py:71
  188.0 14.1 %collective-permute-start.1 = (bf16[3,1,40,2048]{3,2,0,1:T(8,128)(2,1)S(1)}, bf16[3,1,40,2048]{3,2,0,1:T(8,128)(2,1)S(1)}, u32[]{:S(2)}, u32[]{:S(2)}) collective-permute-start(bf16[3,1,40,2048]{3,2,0,1:T(8,128)(2,1)S(1)} %bitcast.225), channel_id=1, source_target_pairs={{0,4},{2,6},{4,0},{6,2},{8,12},{10,14},{12,8},{14,10},{16,20},{18,... | collective-permute-start | bytes 1474568 | tf_op jit(solution)/shard_map/ppermute | solution.py:71
  189.7 22.1 %collective-permute-start.2 = (bf16[3,1,40,2048]{3,2,0,1:T(8,128)(2,1)S(1)}, bf16[3,1,40,2048]{3,2,0,1:T(8,128)(2,1)S(1)}, u32[]{:S(2)}, u32[]{:S(2)}) collective-permute-start(bf16[3,1,40,2048]{3,2,0,1:T(8,128)(2,1)S(1)} %bitcast.222), channel_id=1, source_target_pairs={{0,6},{2,4},{4,2},{6,0},{8,14},{10,12},{12,10},{14,8},{16,22},{18,... | collective-permute-start | bytes 1474568 | tf_op jit(solution)/shard_map/ppermute | solution.py:71
  189.9 25.5 %collective-permute-start.3 = (bf16[3,1,40,2048]{3,2,0,1:T(8,128)(2,1)S(1)}, bf16[3,1,40,2048]{3,2,0,1:T(8,128)(2,1)S(1)}, u32[]{:S(2)}, u32[]{:S(2)}) collective-permute-start(bf16[3,1,40,2048]{3,2,0,1:T(8,128)(2,1)S(1)} %bitcast.220), channel_id=1, source_target_pairs={{0,8},{2,10},{4,12},{6,14},{8,0},{10,2},{12,4},{14,6},{16,24},{18,... | collective-permute-start | bytes 1474568 | tf_op jit(solution)/shard_map/ppermute | solution.py:71
  191.6 24.7 %collective-permute-start.4 = (bf16[3,1,40,2048]{3,2,0,1:T(8,128)(2,1)S(1)}, bf16[3,1,40,2048]{3,2,0,1:T(8,128)(2,1)S(1)}, u32[]{:S(2)}, u32[]{:S(2)}) collective-permute-start(bf16[3,1,40,2048]{3,2,0,1:T(8,128)(2,1)S(1)} %bitcast.218), channel_id=1, source_target_pairs={{0,10},{2,8},{4,14},{6,12},{8,2},{10,0},{12,6},{14,4},{16,26},{18,... | collective-permute-start | bytes 1474568 | tf_op jit(solution)/shard_map/ppermute | solution.py:71
  196.5 50.8 %collective-permute-start.5 = (bf16[3,1,40,2048]{3,2,0,1:T(8,128)(2,1)S(1)}, bf16[3,1,40,2048]{3,2,0,1:T(8,128)(2,1)S(1)}, u32[]{:S(2)}, u32[]{:S(2)}) collective-permute-start(bf16[3,1,40,2048]{3,2,0,1:T(8,128)(2,1)S(1)} %bitcast.223), channel_id=1, source_target_pairs={{0,12},{2,14},{4,8},{6,10},{8,4},{10,6},{12,0},{14,2},{16,28},{18,... | collective-permute-start | bytes 1474568 | tf_op jit(solution)/shard_map/ppermute | solution.py:71
  202.1 54.5 %collective-permute-start.6 = (bf16[3,1,40,2048]{3,2,0,1:T(8,128)(2,1)S(1)}, bf16[3,1,40,2048]{3,2,0,1:T(8,128)(2,1)S(1)}, u32[]{:S(2)}, u32[]{:S(2)}) collective-permute-start(bf16[3,1,40,2048]{3,2,0,1:T(8,128)(2,1)S(1)} %bitcast.221), channel_id=1, source_target_pairs={{0,14},{2,12},{4,10},{6,8},{8,6},{10,4},{12,2},{14,0},{16,30},{18,... | collective-permute-start | bytes 1474568 | tf_op jit(solution)/shard_map/ppermute | solution.py:71
  211.8 47.0 %collective-permute-start.7 = (bf16[3,1,40,2048]{3,2,0,1:T(8,128)(2,1)S(1)}, bf16[3,1,40,2048]{3,2,0,1:T(8,128)(2,1)S(1)}, u32[]{:S(2)}, u32[]{:S(2)}) collective-permute-start(bf16[3,1,40,2048]{3,2,0,1:T(8,128)(2,1)S(1)} %bitcast.219), channel_id=1, source_target_pairs={{0,16},{2,18},{4,20},{6,22},{8,24},{10,26},{12,28},{14,30},{16,0},... | collective-permute-start | bytes 1474568 | tf_op jit(solution)/shard_map/ppermute | solution.py:71
  215.4 46.4 %collective-permute-start.8 = (bf16[3,1,40,2048]{3,2,0,1:T(8,128)(2,1)S(1)}, bf16[3,1,40,2048]{3,2,0,1:T(8,128)(2,1)S(1)}, u32[]{:S(2)}, u32[]{:S(2)}) collective-permute-start(bf16[3,1,40,2048]{3,2,0,1:T(8,128)(2,1)S(1)} %bitcast.217), channel_id=1, source_target_pairs={{0,18},{2,16},{4,22},{6,20},{8,26},{10,24},{12,30},{14,28},{16,2},... | collective-permute-start | bytes 1474568 | tf_op jit(solution)/shard_map/ppermute | solution.py:71
  216.3 106.3 %collective-permute-start.9 = (bf16[3,1,40,2048]{3,2,0,1:T(8,128)(2,1)S(1)}, bf16[3,1,40,2048]{3,2,0,1:T(8,128)(2,1)S(1)}, u32[]{:S(2)}, u32[]{:S(2)}) collective-permute-start(bf16[3,1,40,2048]{3,2,0,1:T(8,128)(2,1)S(1)} %bitcast.216), channel_id=1, source_target_pairs={{0,20},{2,22},{4,16},{6,18},{8,28},{10,30},{12,24},{14,26},{16,4},... | collective-permute-start | bytes 1474568 | tf_op jit(solution)/shard_map/ppermute | solution.py:71
  247.3 95.7 %collective-permute-start.10 = (bf16[3,1,40,2048]{3,2,0,1:T(8,128)(2,1)S(1)}, bf16[3,1,40,2048]{3,2,0,1:T(8,128)(2,1)S(1)}, u32[]{:S(2)}, u32[]{:S(2)}) collective-permute-start(bf16[3,1,40,2048]{3,2,0,1:T(8,128)(2,1)S(1)} %bitcast.215), channel_id=1, source_target_pairs={{0,22},{2,20},{4,18},{6,16},{8,30},{10,28},{12,26},{14,24},{16,6},... | collective-permute-start | bytes 1474568 | tf_op jit(solution)/shard_map/ppermute | solution.py:71
  256.6 87.3 %collective-permute-start.11 = (bf16[3,1,40,2048]{3,2,0,1:T(8,128)(2,1)S(1)}, bf16[3,1,40,2048]{3,2,0,1:T(8,128)(2,1)S(1)}, u32[]{:S(2)}, u32[]{:S(2)}) collective-permute-start(bf16[3,1,40,2048]{3,2,0,1:T(8,128)(2,1)S(1)} %bitcast.214), channel_id=1, source_target_pairs={{0,24},{2,26},{4,28},{6,30},{8,16},{10,18},{12,20},{14,22},{16,8},... | collective-permute-start | bytes 1474568 | tf_op jit(solution)/shard_map/ppermute | solution.py:71
  258.8 85.9 %collective-permute-start.12 = (bf16[3,1,40,2048]{3,2,0,1:T(8,128)(2,1)S(1)}, bf16[3,1,40,2048]{3,2,0,1:T(8,128)(2,1)S(1)}, u32[]{:S(2)}, u32[]{:S(2)}) collective-permute-start(bf16[3,1,40,2048]{3,2,0,1:T(8,128)(2,1)S(1)} %bitcast.213), channel_id=1, source_target_pairs={{0,26},{2,24},{4,30},{6,28},{8,18},{10,16},{12,22},{14,20},{16,10}... | collective-permute-start | bytes 1474568 | tf_op jit(solution)/shard_map/ppermute | solution.py:71
  261.8 83.7 %collective-permute-start.13 = (bf16[3,1,40,2048]{3,2,0,1:T(8,128)(2,1)S(1)}, bf16[3,1,40,2048]{3,2,0,1:T(8,128)(2,1)S(1)}, u32[]{:S(2)}, u32[]{:S(2)}) collective-permute-start(bf16[3,1,40,2048]{3,2,0,1:T(8,128)(2,1)S(1)} %bitcast.212), channel_id=1, source_target_pairs={{0,28},{2,30},{4,24},{6,26},{8,20},{10,22},{12,16},{14,18},{16,12}... | collective-permute-start | bytes 1474568 | tf_op jit(solution)/shard_map/ppermute | solution.py:71
  322.6 23.7 %collective-permute-start.14 = (bf16[3,1,40,2048]{3,2,0,1:T(8,128)(2,1)S(1)}, bf16[3,1,40,2048]{3,2,0,1:T(8,128)(2,1)S(1)}, u32[]{:S(2)}, u32[]{:S(2)}) collective-permute-start(bf16[3,1,40,2048]{3,2,0,1:T(8,128)(2,1)S(1)} %bitcast.211), channel_id=1, source_target_pairs={{0,30},{2,28},{4,26},{6,24},{8,22},{10,20},{12,18},{14,16},{16,14}... | collective-permute-start | bytes 1474568 | tf_op jit(solution)/shard_map/ppermute | solution.py:71
  527.2 69.6 %copy-start.27 = (f32[2048]{0:T(1024)S(1)}, f32[2048]{0:T(1024)}, u32[]{:S(2)}) copy-start(f32[2048]{0:T(1024)} %param.11) | copy-start | bytes 24580
  769.6 4.7 copy-start.23
  785.7 4.6 copy-start.16
  788.0 4.6 copy-start.15
  790.3 4.6 copy-start.14
  803.9 5.5 copy-start.10
  803.9 5.6 copy-start.7
  803.9 5.7 copy-start.6
  803.9 5.8 copy-start.4
  803.9 5.9 copy-start.3
  803.9 6.0 copy-start.2
  805.1 5.0 copy-start.1
  (15 other events, 58.3 us)
Sparse Core Ops, SparseCore 0:
  530.7 164.3 all-gather.2
